TPU v7x, 512 devices: a whole 4x8x8 slice. The times are simulated.
512 devices in a mesh: section: 2 (over z_lo), batch: 16 (over z_hi, x), tensor: 16 (over y, core).
Axes of the slice: x: 4, y: 8, z: 8 (z_hi: 4, z_lo: 2; z = z_hi * 2 + z_lo), core: 2. Of those that a mesh axis runs over, the one named last changes fastest.
Arguments:
- tokens: bfloat16 [4096, 4096], P('batch', ('section', 'tensor')), may hold values from -950 to 950, as said below
- nb_ids: int32 [128, 128], P('batch'), may hold values from 0 to 15999
- nb_index: int32 [64, 2], P('batch'), may hold values from 0 to 7
- table: bfloat16 [16000, 4096], P('batch', ('section', 'tensor')), may hold values from -950 to 950, as said below
- norm_gains: float32 [2, 4096], replicated, may hold values from 0.1 to 1.9
- projections: bfloat16 [2, 2, 4096, 4096], P(None, None, None, ('section', 'tensor')), may hold values from -0.5 to 0.5
Outputs:
- mixed: bfloat16 [4096, 4096], P('batch', ('section', 'tensor'))
Inputs may be any that keep to these rules, and one draw needn't show every extreme that they name: tokens: entries of order one to some hundreds, of both signs. table: entries of order one to some hundreds, of both signs.
All inputs are finite; a program needn't handle non-finite values.
Results may differ from a plain program's by a relative error of at most 0.019.
Values may be sent and summed in bfloat16 or wider, within the bound.
No kernel may reach another device: no remote copies, remote signals or barrier semaphores. Data moves between devices by JAX's collectives and lax.ppermute only.
A program may use at most 64 MiB of HBM per device.

v0:
```python
import math
import jax
import jax.numpy as jnp
from jax import lax
from jax.sharding import PartitionSpec as P

HEAD_DIM = 128
SPAN = 64
NEIGH = 2


def rms_norm(values, gain):
    wide = values.astype(jnp.float32)
    square = jnp.mean(wide * wide, axis=-1, keepdims=True)
    return (wide * lax.rsqrt(square + 1e-06) * gain).astype(jnp.bfloat16)


def on_device(tokens, nb_ids, nb_index, table, norm_gains, projections):
    piece_cols = table.shape[1]
    block_count, neighbour_len = nb_ids.shape
    nb_rows = block_count * neighbour_len
    flat_ids = nb_ids.reshape(nb_rows)
    piece = lax.all_gather(table, "batch", axis=0, tiled=True)
    inside = (flat_ids >= 0) & (flat_ids < piece.shape[0])
    picked = jnp.take(piece, jnp.clip(flat_ids, 0, piece.shape[0] - 1), axis=0)
    embedded = jnp.where(inside[:, None], picked, jnp.zeros((nb_rows, piece_cols), jnp.bfloat16))
    full_neighbours = lax.all_gather(embedded, ("section", "tensor"), axis=1, tiled=True)
    encoded = rms_norm(full_neighbours, norm_gains[0])
    key_value = jnp.einsum(
        "md,jdc->jmc", encoded, projections[0], preferred_element_type=jnp.float32
    ).astype(jnp.bfloat16)
    full_tokens = lax.all_gather(tokens, ("section", "tensor"), axis=1, tiled=True)
    normed = rms_norm(full_tokens, norm_gains[1])
    queries = jnp.dot(normed, projections[1, 0], preferred_element_type=jnp.float32).astype(
        jnp.bfloat16
    )
    tok_rows, head_cols = queries.shape
    local_heads = head_cols // HEAD_DIM
    span_count = tok_rows // SPAN
    query_blocks = queries.reshape(span_count, SPAN, local_heads, HEAD_DIM)
    stacked = key_value.reshape(2, block_count, neighbour_len, local_heads, HEAD_DIM)
    chosen = stacked[:, nb_index].reshape(
        2, span_count, NEIGH * neighbour_len, local_heads, HEAD_DIM
    )
    scores = jnp.einsum(
        "cqhd,ckhd->chqk", query_blocks, chosen[0], preferred_element_type=jnp.float32
    ) * (1.0 / math.sqrt(HEAD_DIM))
    expo = jnp.exp(scores)
    weights = (expo / jnp.sum(expo, axis=-1, keepdims=True)).astype(jnp.bfloat16)
    attended = jnp.einsum("chqk,ckhd->cqhd", weights, chosen[1], preferred_element_type=jnp.float32)
    attended = attended.astype(jnp.bfloat16).reshape(tok_rows, head_cols)
    out_weight = projections[1, 1]
    width = out_weight.shape[0]
    tensor_count = lax.axis_size("tensor")
    out_cols = width // (2 * tensor_count)
    grid = out_weight.reshape(2, tensor_count, out_cols, head_cols)
    partial_sums = jnp.einsum(
        "rh,stch->rtsc", attended, grid, preferred_element_type=jnp.float32
    ).reshape(tok_rows, width)
    within = lax.psum_scatter(
        partial_sums.astype(jnp.bfloat16), "tensor", scatter_dimension=1, tiled=True
    )
    result = lax.psum_scatter(within, "section", scatter_dimension=1, tiled=True).astype(
        jnp.float32
    )
    return result.astype(jnp.bfloat16)


def solution(mesh):
    return jax.shard_map(
        on_device,
        mesh=mesh,
        in_specs=(
            P("batch", ("section", "tensor")),
            P("batch", None),
            P("batch", None),
            P("batch", ("section", "tensor")),
            P(),
            P(None, None, None, ("section", "tensor")),
        ),
        out_specs=P("batch", ("section", "tensor")),
        check_vma=False,
    )
```

profile of v0, /device:TPU:1, one launch (start us, length us, event | category | flops | bytes accessed | tf_op | source)
XLA Modules:
  0.0 360.7 jit_solution(11192853730899416732)
XLA Ops:
  6.5 0.0 copy-start.1
  6.5 0.0 all-gather.4.cloned.1.call-start
  6.5 0.7 all-gather.4.cloned.1.call-update
  7.3 0.0 all-gather.8.cloned.1.call-start
  7.3 0.7 all-gather.8.cloned.1.call-update
  8.0 0.0 all-gather.6.cloned.1.call-start
  8.1 0.7 and_bitcast_fusion
  8.7 0.7 compare_and_fusion
  9.4 0.7 broadcast_clamp_fusion.1
  10.2 87.7 %all-gather.4.cloned.1.call-done = bf16[16000,128]{1,0:T(8,128)(2,1)} async-done(((bf16[1000,128]{1,0:T(8,128)(2,1)}), bf16[16000,128]{1,0:T(8,128)(2,1)}) %all-gather.4.cloned.1.call-update) | async-done | bytes 4096016 | tf_op jit(solution)/shard_map/all_gather | solution.py:23
  97.9 5.6 %gather_fusion = bf16[1024,128]{1,0:T(8,128)(2,1)S(1)} fusion(bf16[16000,128]{1,0:T(8,128)(2,1)} %all-gather.4.cloned.1.call-done, s32[1024]{0:T(1024)S(1)} %broadcast_clamp_fusion), kind=kCustom, calls=%fused_computation | custom fusion | bytes 528384 | tf_op jit(solution)/shard_map/jit(_take)/gather | solution.py:25
  103.4 1.0 select_select_fusion
  104.5 0.0 all-gather.6.cloned.1.call-update
  104.5 0.0 reduce-scatter.3.cloned.1.call-start
  104.6 0.7 compare_select_fusion.2
  105.2 0.1 copy.9
  105.3 0.1 reshape.120
  105.4 1.3 slice.29
  106.7 0.0 copy-done.1
  106.8 61.8 %all-gather.8.cloned.1.call-done = bf16[256,4096]{1,0:T(8,128)(2,1)} async-done(((bf16[256,128]{1,0:T(8,128)(2,1)}), bf16[256,4096]{1,0:T(8,128)(2,1)}) %all-gather.8.cloned.1.call-update) | async-done | bytes 2097168 | tf_op jit(solution)/shard_map/all_gather | solution.py:32
  168.5 2.1 fusion.6
  170.6 2.7 fusion.21
  173.3 85.6 %all-gather.6.cloned.1.call-done = bf16[1024,4096]{1,0:T(8,128)(2,1)} async-done(((bf16[1024,128]{1,0:T(8,128)(2,1)}), bf16[1024,4096]{1,0:T(8,128)(2,1)}) %all-gather.6.cloned.1.call-update) | async-done | bytes 8388624 | tf_op jit(solution)/shard_map/all_gather | solution.py:27
  258.9 0.0 copy-start
  258.9 5.2 %fusion = f32[1024]{0:T(1024)S(1)} fusion(bf16[1024,4096]{1,0:T(8,128)(2,1)} %all-gather.6.cloned.1.call-done), kind=kLoop, calls=%fused_computation.4 | loop fusion | flops 12581888 | bytes 8392704 | tf_op jit(solution)/shard_map/reduce_sum | solution.py:14
  264.2 0.5 copy-done
  264.7 4.0 %fusion.15 = bf16[1024,2,128]{2,0,1:T(8,128)(2,1)S(1)} fusion(bf16[2,2,4096,128]{3,2,1,0:T(8,128)(2,1)} %param.11, bf16[1024,4096]{1,0:T(8,128)(2,1)S(1)} %copy-done, f32[4096]{0:T(1024)S(1)} %bitcast.63, f32[1024]{0:T(1024)S(1)} %add_rsqrt_fusion), kind=kOutput, calls=%fused_computation.20 | convolution fusion | flops 2164523008 | bytes 11030528 | tf_op jit(solution)/shard_map/md,jdc->jmc/dot_general | solution.py:29
  268.8 0.6 gather_fusion.1
  269.5 0.2 fusion.20
  269.7 0.2 convolution_convert_fusion
  270.0 0.7 convert_bitcast_fusion
  270.7 1.5 copy.11
  272.2 0.0 reduce-scatter.3.cloned.1.call-update
  272.2 0.0 reduce-scatter.5.cloned.1.call-start
  272.2 58.8 %reduce-scatter.3.cloned.1.call-done = bf16[256,256]{0,1:T(8,128)(2,1)} async-done(((bf16[256,4096]{0,1:T(8,128)(2,1)}), bf16[256,256]{0,1:T(8,128)(2,1)}) %reduce-scatter.3.cloned.1.call-update) | async-done | bytes 131088 | tf_op jit(solution)/shard_map/reduce_scatter | solution.py:60
  331.0 0.0 reduce-scatter.5.cloned.1.call-update
  331.1 21.5 %reduce-scatter.5.cloned.1.call-done = bf16[256,128]{0,1:T(8,128)(2,1)} async-done(((bf16[256,256]{0,1:T(8,128)(2,1)}), bf16[256,128]{0,1:T(8,128)(2,1)}) %reduce-scatter.5.cloned.1.call-update) | async-done | bytes 65552 | tf_op jit(solution)/shard_map/reduce_scatter | solution.py:63
  352.6 1.6 copy.12
  (8 shorter events, 0.1 us)
Async XLA Ops:
  6.5 100.2 %copy-start.1 = (f32[2,4096]{1,0:T(2,128)S(1)}, f32[2,4096]{1,0:T(2,128)}, u32[]{:S(2)}) copy-start(f32[2,4096]{1,0:T(2,128)} %param.10) | copy-start | bytes 98308
  6.5 91.3 %all-gather.4.cloned.1.call-start = ((), (), s32[]{:S(2)}) async-start(), calls=%async_computation.2 | async-start | bytes 4352000 | tf_op jit(solution)/shard_map/all_gather | solution.py:23
  7.3 161.3 %all-gather.8.cloned.1.call-start = ((), (), s32[]{:S(2)}) async-start(), calls=%async_computation.4 | async-start | bytes 2162688 | tf_op jit(solution)/shard_map/all_gather | solution.py:32
  8.0 250.9 %all-gather.6.cloned.1.call-start = ((), (), s32[]{:S(2)}) async-start(), calls=%async_computation.3 | async-start | bytes 8650752 | tf_op jit(solution)/shard_map/all_gather | solution.py:27
  104.5 226.5 %reduce-scatter.3.cloned.1.call-start = ((), (), s32[]{:S(2)}) async-start(), calls=%async_computation.5 | async-start | bytes 2228224 | tf_op jit(solution)/shard_map/reduce_scatter | solution.py:60
  258.9 5.8 %copy-start = (bf16[1024,4096]{1,0:T(8,128)(2,1)S(1)}, bf16[1024,4096]{1,0:T(8,128)(2,1)}, u32[]{:S(2)}) copy-start(bf16[1024,4096]{1,0:T(8,128)(2,1)} %all-gather.6.cloned.1.call-done) | copy-start | bytes 25165828
  272.2 80.4 %reduce-scatter.5.cloned.1.call-start = ((), (), s32[]{:S(2)}) async-start(), calls=%async_computation.6 | async-start | bytes 196608 | tf_op jit(solution)/shard_map/reduce_scatter | solution.py:63
Sparse Core Ops, SparseCore 0:
  10.4 87.4 all-gather.3
  99.9 68.5 all-gather.7
  170.6 88.2 all-gather.5
  272.3 58.6 reduce-scatter.2
  333.6 18.8 reduce-scatter.4
where the time goes:
time: 361 us
  waiting for transfers between devices  317 us (88%)
  between operations  13.2 us (4%)
  local copies, waits for them, and re-layouts  11.4 us (3%)
  other arithmetic  11.1 us (3%)
  matrix products  7.87 us (2%)
    all_gather x1, waiting for transfers between devices, on_device(): piece = lax.all_gather(table, 'batch', axis=0, tiled=True)  87.7 us
    all_gather x1, waiting for transfers between devices, on_device(): lax.all_gather(embedded, ('section', 'tensor'), axis=1, tiled=True)  85.6 us
    all_gather x1, waiting for transfers between devices, on_device(): lax.all_gather(tokens, ('section', 'tensor'), axis=1, tiled=True)  61.8 us
    reduce_scatter x1, waiting for transfers between devices, on_device(): lax.psum_scatter(partial_sums.astype(jnp.bfloat16), 'tensor', scatter_dim...  58.8 us
    reduce_scatter x1, waiting for transfers between devices, on_device(): lax.psum_scatter(within, 'section', scatter_dimension=1, tiled=True)  21.5 us
    reduce_sum x2, other arithmetic, rms_norm(): square = jnp.mean(wide * wide, axis=-1, keepdims=True)  7.3 us
  transfers between devices with their start and end apart: 5, of which 5 were waited for; matrix products, arithmetic and copies ran while one was open for 4% of the time, Pallas kernels for 0%

commit v1 on v0

--- a/solution.py
+++ b/solution.py
@@ -29,7 +29,12 @@
     key_value = jnp.einsum(
         "md,jdc->jmc", encoded, projections[0], preferred_element_type=jnp.float32
     ).astype(jnp.bfloat16)
-    full_tokens = lax.all_gather(tokens, ("section", "tensor"), axis=1, tiled=True)
+    full_tokens = jnp.concatenate(
+        lax.all_to_all(
+            jnp.stack([tokens] * lax.axis_size(("section", "tensor"))), ("section", "tensor"), 0, 0
+        ),
+        axis=1,
+    )
     normed = rms_norm(full_tokens, norm_gains[1])
     queries = jnp.dot(normed, projections[1, 0], preferred_element_type=jnp.float32).astype(
         jnp.bfloat16

time: 361 us -> 330 us (0.914)
  waiting for transfers between devices: 317 us -> 277 us
  starting transfers between devices: 0.16 us -> 8.93 us
    all_gather x1 -> x0, waiting for transfers between devices: 61.8 us -> none  [on_device(): lax.all_gather(tokens, ('section', 'tensor'), axis=1, tiled=True)]
    all_to_all x0 -> x1, waiting for transfers between devices: none -> 60 us  [on_device(): lax.all_to_all(jnp.stack([tokens] * lax.axis_size(('section', 'tensor')))...]
    all_gather x1, waiting for transfers between devices: 85.6 us -> 49.3 us  [on_device(): lax.all_gather(embedded, ('section', 'tensor'), axis=1, tiled=True)]
    all_to_all x0 -> x1, starting transfers between devices: none -> 8.8 us  [on_device(): lax.all_to_all(jnp.stack([tokens] * lax.axis_size(('section', 'tensor')))...]
  transfers between devices with their start and end apart: 5 -> 5, of which waited for: 5 -> 5; matrix products, arithmetic and copies ran while one was open for 4% -> 3% of each run, Pallas kernels for 0% -> 0%
where the time goes in v1:
time: 330 us
  waiting for transfers between devices  277 us (84%)
  local copies, waits for them, and re-layouts  13.9 us (4%)
  between operations  13.3 us (4%)
  other arithmetic  9.68 us (3%)
  starting transfers between devices  8.93 us (3%)
  matrix products  7.2 us (2%)
    all_gather x1, waiting for transfers between devices, on_device(): piece = lax.all_gather(table, 'batch', axis=0, tiled=True)  88.5 us
    all_to_all x1, waiting for transfers between devices, on_device(): lax.all_to_all(jnp.stack([tokens] * lax.axis_size(('section', 'tensor')))...  60 us
    reduce_scatter x1, waiting for transfers between devices, on_device(): lax.psum_scatter(partial_sums.astype(jnp.bfloat16), 'tensor', scatter_dim...  56.8 us
    all_gather x1, waiting for transfers between devices, on_device(): lax.all_gather(embedded, ('section', 'tensor'), axis=1, tiled=True)  49.3 us
    reduce_scatter x1, waiting for transfers between devices, on_device(): lax.psum_scatter(within, 'section', scatter_dimension=1, tiled=True)  21.5 us
    all_to_all x1, starting transfers between devices, on_device(): lax.all_to_all(jnp.stack([tokens] * lax.axis_size(('section', 'tensor')))...  8.8 us
  transfers between devices with their start and end apart: 5, of which 5 were waited for; matrix products, arithmetic and copies ran while one was open for 3% of the time, Pallas kernels for 0%

profile of v1, /device:TPU:1, one launch (start us, length us, event | category | flops | bytes accessed | tf_op | source)
XLA Modules:
  0.0 329.8 jit_solution(16381598644253557920)
XLA Ops:
  6.5 0.0 all-gather.3.cloned.1.call-start
  6.5 0.7 all-gather.3.cloned.1.call-update
  7.3 0.0 all-gather.5.cloned.1.call-start
  7.3 0.7 and_bitcast_fusion
  8.0 0.7 compare_and_fusion
  8.7 0.7 broadcast_clamp_fusion.1
  9.4 88.5 %all-gather.3.cloned.1.call-done = bf16[16000,128]{1,0:T(8,128)(2,1)} async-done(((bf16[1000,128]{1,0:T(8,128)(2,1)}), bf16[16000,128]{1,0:T(8,128)(2,1)}) %all-gather.3.cloned.1.call-update) | async-done | bytes 4096016 | tf_op jit(solution)/shard_map/all_gather | solution.py:23
  97.9 5.6 %gather_fusion = bf16[1024,128]{1,0:T(8,128)(2,1)S(1)} fusion(bf16[16000,128]{1,0:T(8,128)(2,1)} %all-gather.3.cloned.1.call-done, s32[1024]{0:T(1024)S(1)} %broadcast_clamp_fusion), kind=kCustom, calls=%fused_computation | custom fusion | bytes 528384 | tf_op jit(solution)/shard_map/jit(_take)/gather | solution.py:25
  103.4 0.0 copy-start.2
  103.4 1.0 select_select_fusion
  104.5 0.0 all-gather.5.cloned.1.call-update
  104.5 0.9 copy.11
  105.5 0.0 copy-start.1
  105.5 1.6 stack.2
  107.1 8.8 %all-to-all-start = ((bf16[32,256,128]{1,2,0:T(8,128)(2,1)}), bf16[32,256,128]{1,2,0:T(8,128)(2,1)S(1)}, u32[]{:S(2)}, u32[]{:S(2)}) async-start(bf16[32,256,128]{1,2,0:T(8,128)(2,1)} %stack.2), calls=%async_computation | async-start | bytes 4194304 | tf_op jit(solution)/shard_map/all_to_all | solution.py:33
  115.9 0.0 reduce-scatter.3.cloned.1.call-start
  115.9 0.0 copy-done.2
  115.9 0.1 copy.9
  116.0 0.1 reshape.135
  116.1 1.3 slice.29
  117.4 0.0 copy-done.1
  117.5 60.0 %all-to-all-done = bf16[32,256,128]{1,2,0:T(8,128)(2,1)S(1)} async-done(((bf16[32,256,128]{1,2,0:T(8,128)(2,1)}), bf16[32,256,128]{1,2,0:T(8,128)(2,1)S(1)}, u32[]{:S(2)}, u32[]{:S(2)}) %all-to-all-start) | async-done | bytes 2097184 | tf_op jit(solution)/shard_map/all_to_all | solution.py:33
  177.4 0.6 fusion.6
  178.0 0.7 fusion.8
  178.8 2.0 convolution_convert_fusion
  180.8 49.3 %all-gather.5.cloned.1.call-done = bf16[1024,4096]{1,0:T(8,128)(2,1)} async-done(((bf16[1024,128]{1,0:T(8,128)(2,1)}), bf16[1024,4096]{1,0:T(8,128)(2,1)}) %all-gather.5.cloned.1.call-update) | async-done | bytes 8388624 | tf_op jit(solution)/shard_map/all_gather | solution.py:27
  230.0 0.0 copy-start
  230.0 5.2 %fusion = f32[1024]{0:T(1024)S(1)} fusion(bf16[1024,4096]{1,0:T(8,128)(2,1)} %all-gather.5.cloned.1.call-done), kind=kLoop, calls=%fused_computation.4 | loop fusion | flops 12581888 | bytes 8392704 | tf_op jit(solution)/shard_map/reduce_sum | solution.py:14
  235.3 0.5 copy-done
  235.8 4.0 %fusion.11 = bf16[1024,2,128]{2,0,1:T(8,128)(2,1)S(1)} fusion(bf16[2,2,4096,128]{3,2,1,0:T(8,128)(2,1)} %param.11, bf16[1024,4096]{1,0:T(8,128)(2,1)S(1)} %copy-done, f32[4096]{0:T(1024)S(1)} %bitcast.69, f32[1024]{0:T(1024)S(1)} %add_rsqrt_fusion), kind=kOutput, calls=%fused_computation.17 | convolution fusion | flops 2164523008 | bytes 11030528 | tf_op jit(solution)/shard_map/md,jdc->jmc/dot_general | solution.py:29
  239.9 0.6 gather_fusion.1
  240.6 0.2 fusion.16
  240.8 0.2 convolution_convert_fusion.1
  241.1 0.7 convert_bitcast_fusion
  241.8 1.5 copy.12
  243.3 0.0 reduce-scatter.3.cloned.1.call-update
  243.3 0.0 reduce-scatter.5.cloned.1.call-start
  243.3 56.8 %reduce-scatter.3.cloned.1.call-done = bf16[256,256]{0,1:T(8,128)(2,1)} async-done(((bf16[256,4096]{0,1:T(8,128)(2,1)}), bf16[256,256]{0,1:T(8,128)(2,1)}) %reduce-scatter.3.cloned.1.call-update) | async-done | bytes 131088 | tf_op jit(solution)/shard_map/reduce_scatter | solution.py:65
  300.1 0.0 reduce-scatter.5.cloned.1.call-update
  300.2 21.5 %reduce-scatter.5.cloned.1.call-done = bf16[256,128]{0,1:T(8,128)(2,1)} async-done(((bf16[256,256]{0,1:T(8,128)(2,1)}), bf16[256,128]{0,1:T(8,128)(2,1)}) %reduce-scatter.5.cloned.1.call-update) | async-done | bytes 65552 | tf_op jit(solution)/shard_map/reduce_scatter | solution.py:68
  321.7 1.6 copy.13
  (9 shorter events, 0.2 us)
Async XLA Ops:
  6.5 91.3 %all-gather.3.cloned.1.call-start = ((), (), s32[]{:S(2)}) async-start(), calls=%async_computation.3 | async-start | bytes 4352000 | tf_op jit(solution)/shard_map/all_gather | solution.py:23
  7.3 222.8 %all-gather.5.cloned.1.call-start = ((), (), s32[]{:S(2)}) async-start(), calls=%async_computation.4 | async-start | bytes 8650752 | tf_op jit(solution)/shard_map/all_gather | solution.py:27
  103.4 12.5 %copy-start.2 = (s32[4,2]{0,1:T(2,128)S(1)}, s32[4,2]{0,1:T(2,128)}, u32[]{:S(2)}) copy-start(s32[4,2]{0,1:T(2,128)} %param.8) | copy-start | bytes 100
  105.5 12.0 %copy-start.1 = (f32[2,4096]{1,0:T(2,128)S(1)}, f32[2,4096]{1,0:T(2,128)}, u32[]{:S(2)}) copy-start(f32[2,4096]{1,0:T(2,128)} %param.10) | copy-start | bytes 98308
  107.1 70.4 %all-to-all-start = ((bf16[32,256,128]{1,2,0:T(8,128)(2,1)}), bf16[32,256,128]{1,2,0:T(8,128)(2,1)S(1)}, u32[]{:S(2)}, u32[]{:S(2)}) async-start(bf16[32,256,128]{1,2,0:T(8,128)(2,1)} %stack.2), calls=%async_computation | async-start | bytes 4194304 | tf_op jit(solution)/shard_map/all_to_all | solution.py:33
  115.9 184.3 %reduce-scatter.3.cloned.1.call-start = ((), (), s32[]{:S(2)}) async-start(), calls=%async_computation.5 | async-start | bytes 2228224 | tf_op jit(solution)/shard_map/reduce_scatter | solution.py:65
  230.0 5.8 %copy-start = (bf16[1024,4096]{1,0:T(8,128)(2,1)S(1)}, bf16[1024,4096]{1,0:T(8,128)(2,1)}, u32[]{:S(2)}) copy-start(bf16[1024,4096]{1,0:T(8,128)(2,1)} %all-gather.5.cloned.1.call-done) | copy-start | bytes 25165828
  243.3 78.4 %reduce-scatter.5.cloned.1.call-start = ((), (), s32[]{:S(2)}) async-start(), calls=%async_computation.6 | async-start | bytes 196608 | tf_op jit(solution)/shard_map/reduce_scatter | solution.py:68
Sparse Core Ops, SparseCore 0:
  10.4 87.4 all-gather.2
  104.6 125.3 all-gather.4
  243.4 56.6 reduce-scatter.2
  302.7 18.8 reduce-scatter.4
